TPU v7x, 32 devices: a whole 2x2x4 slice. The times are simulated.
32 devices in a mesh: orb: 8 (over y, x, core), aux: 4 (over z).
Axes of the slice: x: 2, y: 2, z: 4, core: 2. Of those that a mesh axis runs over, the one named last changes fastest.
Arguments:
- blocks: bfloat16 [32, 256, 6144], P('orb', None, 'aux'), may hold values from -0.65625 to 0.65625
- excitation: float32 [32, 256], replicated, may hold values from 0.5 to 8
- partner: int32 [8, 8], replicated, may hold values from 0 to 3
- neighbours: int32 [8, 8], replicated, may hold values from 0 to 1, as said below
Outputs:
- gradient: bfloat16 [32, 256, 6144], P('orb', None, 'aux')
Inputs may be any that keep to these rules, and one draw needn't show every extreme that they name: neighbours is symmetric: neighbours[d][s] equals neighbours[s][d].
All inputs are finite; a program needn't handle non-finite values.
Results may differ from a plain program's by a relative error of at most 0.0048.
Values may be sent and summed in bfloat16 or wider, within the bound.
No kernel may reach another device: no remote copies, remote signals or barrier semaphores. Data moves between devices by JAX's collectives and lax.ppermute only.
A program may use at most 192 MiB of HBM per device.

v0:
```python
import jax
import jax.numpy as jnp
from jax import lax
from jax.sharding import PartitionSpec as P


def amplitudes(kernel, own_rows, far_rows, weights, excitation):
    denominator = excitation[own_rows][:, :, None] + excitation[far_rows][:, None, :]
    return (-weights[:, None, None] * kernel / denominator).astype(jnp.bfloat16)


def reduce_amplitudes(kernel_part, own_rows, far_rows, weights, excitation):
    kernel = lax.psum(kernel_part, "aux")
    return amplitudes(kernel, own_rows, far_rows, weights, excitation)


def on_device(blocks, excitation, partner, neighbours):
    peers = lax.axis_size("orb")
    anchor = lax.axis_index("orb")
    local_count = blocks.shape[0]
    width = blocks.shape[1]
    aux_width = blocks.shape[2]
    wanted = partner[:, anchor]
    own_rows = anchor * local_count + wanted
    far_rows = jnp.arange(peers, dtype=jnp.int32) * local_count + partner[anchor, :]
    weights = neighbours[anchor, :].astype(jnp.float32)
    outgoing = jnp.take(blocks, wanted, axis=0)
    received = lax.all_to_all(outgoing, "orb", split_axis=0, concat_axis=0, tiled=True)
    kernel_part = jnp.einsum("sap,sbp->sab", outgoing, received, preferred_element_type=jnp.float32)
    amplitude = reduce_amplitudes(kernel_part, own_rows, far_rows, weights, excitation)
    onehot = (wanted[:, None] == jnp.arange(local_count, dtype=jnp.int32)[None, :]).astype(
        jnp.float32
    )
    grouped = 8
    groups = peers // grouped
    amplitude_groups = amplitude.reshape(groups, grouped, width, width)
    received_groups = received.reshape(groups, grouped, width, aux_width)
    onehot_groups = onehot.reshape(groups, grouped, local_count)

    def accumulate(running, pieces):
        product = jnp.einsum(
            "sab,sbp->sap", pieces[0], pieces[1], preferred_element_type=jnp.float32
        )
        added = jnp.einsum("si,sap->iap", pieces[2], product, precision=lax.Precision.HIGHEST)
        return (running + added, None)

    initial = jnp.zeros((local_count, width, aux_width), jnp.float32)
    running, unused = lax.scan(
        accumulate, initial, (amplitude_groups, received_groups, onehot_groups)
    )
    return running.astype(jnp.bfloat16)


def solution(mesh):
    placed = (P("orb", None, "aux"), P(), P(), P())
    return jax.shard_map(
        on_device, mesh=mesh, in_specs=placed, out_specs=P("orb", None, "aux"), check_vma=False
    )
```

profile of v0, /device:TPU:0, one launch (start us, length us, event | category | flops | bytes accessed | tf_op | source)
XLA Modules:
  0.0 209.4 jit_solution(16170676096387874628)
XLA Ops:
  6.5 0.0 copy-start
  6.5 0.0 all-reduce.2.cloned.1.call-start
  6.5 0.9 constant_dynamic-slice_fusion.2
  7.4 0.1 copy.8
  7.5 0.7 fusion.17
  8.2 0.2 copy-done
  8.4 3.6 %gather_fusion = bf16[8,256,1536]{2,1,0:T(8,128)(2,1)} fusion(bf16[4,256,1536]{2,1,0:T(8,128)(2,1)S(1)} %copy-done, s32[1024]{0:T(1024)S(1)} %pad_clamp_fusion.2), kind=kCustom, calls=%fused_computation | custom fusion | bytes 12582944 | tf_op jit(solution)/shard_map/jit(_take)/gather | solution.py:27
  12.0 3.5 %broadcast_select_fusion = bf16[8,256,1536]{2,1,0:T(8,128)(2,1)S(1)} fusion(bf16[8,256,1536]{2,1,0:T(8,128)(2,1)} %gather_fusion, pred[8]{0:T(512)(128)(4,1)S(1)} %and_bitcast_fusion), kind=kLoop, calls=%fused_computation.5 | loop fusion | flops 3145728 | bytes 12582920 | tf_op jit(solution)/shard_map/jit(_take)/select_n | solution.py:27
  15.5 76.5 %all_to_all.5 = bf16[8,256,1536]{2,1,0:T(8,128)(2,1)S(1)} all-to-all(bf16[8,256,1536]{2,1,0:T(8,128)(2,1)S(1)} %broadcast_select_fusion), channel_id=1, replica_groups=mesh['orb'=8,'aux'=4] {'orb'}, dimensions={0} | all-to-all | bytes 12582912 | tf_op jit(solution)/shard_map/all_to_all | solution.py:28
  92.0 0.0 copy-start.1
  92.0 2.6 %copy-done.1 = bf16[8,256,1536]{2,1,0:T(8,128)(2,1)} copy-done((bf16[8,256,1536]{2,1,0:T(8,128)(2,1)}, bf16[8,256,1536]{2,1,0:T(8,128)(2,1)S(1)}, u32[]{:S(2)}) %copy-start.1) | copy-done | bytes 6291480
  94.7 0.0 copy-start.2
  94.7 3.1 %fusion.20 = f32[8,256,256]{2,1,0:T(8,128)} fusion(bf16[8,256,1536]{2,1,0:T(8,128)(2,1)S(1)} %broadcast_select_fusion, bf16[8,256,1536]{2,1,0:T(8,128)(2,1)S(1)} %all_to_all.5), kind=kOutput, calls=%fused_computation.33 | convolution fusion | flops 1610612736 | bytes 14680064 | tf_op jit(solution)/shard_map/sap,sbp->sab/dot_general | solution.py:29
  97.8 0.0 all-reduce.2.cloned.1.call-update
  97.8 0.0 copy-done.2
  97.8 0.6 gather_fusion.1
  98.4 0.6 gather_fusion.2
  99.0 0.7 fusion.14
  99.7 84.2 %all-reduce.2.cloned.1.call-done = f32[8,256,256]{2,1,0:T(8,128)} async-done(((f32[8,256,256]{2,1,0:T(8,128)}), f32[8,256,256]{2,1,0:T(8,128)}) %all-reduce.2.cloned.1.call-update) | async-done | bytes 2097168 | tf_op jit(solution)/shard_map/psum | solution.py:13
  183.9 5.3 %fusion.5 = f32[8,256,1536]{2,1,0:T(8,128)S(1)} fusion(bf16[8,256,1536]{2,1,0:T(8,128)(2,1)} %copy-done.1, f32[8,256,256]{2,1,0:T(8,128)} %all-reduce.2.cloned.1.call-done, f32[8,256]{1,0:T(8,128)S(1)} %gather_fusion.2, f32[8,256]{1,0:T(8,128)S(1)} %gather_fusion.1, f32[8]{0:T(128)S(1)} %fusion.14), kind=kOutput, calls=%fused_computation.8 | convolution fusion | flops 1612709888 | bytes 20987936 | tf_op jit(solution)/shard_map/while/body/eval_jaxpr/sab,sbp->sap/dot_general | solution.py:41
  189.1 11.2 %fusion.2 = bf16[4,256,1536]{2,0,1:T(4,128)(2,1)S(1)} fusion(f32[8,256,1536]{2,1,0:T(8,128)S(1)} %fusion.5, s32[8]{0:T(128)S(1)} %bitcast.25), kind=kOutput, calls=%fused_computation.6 | convolution fusion | flops 152567840 | bytes 15728672 | tf_op jit(solution)/shard_map/while/body/eval_jaxpr/si,sap->iap/dot_general | solution.py:44
  200.3 2.2 %copy.6 = bf16[4,256,1536]{2,1,0:T(8,128)(2,1)} copy(bf16[4,256,1536]{2,0,1:T(4,128)(2,1)S(1)} %fusion.2) | data formatting | bytes 6291456 | tf_op jit(solution)/shard_map/convert_element_type | solution.py:51
  (4 shorter events, 0.0 us)
Async XLA Ops:
  6.5 1.9 copy-start
  6.5 177.3 %all-reduce.2.cloned.1.call-start = ((), (), s32[]{:S(2)}) async-start(), calls=%async_computation.1 | async-start | bytes 4194304 | tf_op jit(solution)/shard_map/psum | solution.py:13
  92.0 2.7 %copy-start.1 = (bf16[8,256,1536]{2,1,0:T(8,128)(2,1)}, bf16[8,256,1536]{2,1,0:T(8,128)(2,1)S(1)}, u32[]{:S(2)}) copy-start(bf16[8,256,1536]{2,1,0:T(8,128)(2,1)S(1)} %all_to_all.5) | copy-start | bytes 18874372
  94.7 3.2 %copy-start.2 = (f32[32,256]{1,0:T(8,128)S(1)}, f32[32,256]{1,0:T(8,128)}, u32[]{:S(2)}) copy-start(f32[32,256]{1,0:T(8,128)} %param.5) | copy-start | bytes 98308
Sparse Core Ops, SparseCore 0:
  97.9 85.8 all-reduce.1
where the time goes:
time: 210 us; the launch traced here: 209 us
  waiting for transfers between devices  84.2 us (40%)
  blocking collectives  76.5 us (36%)
  matrix products  19.6 us (9%)
  between operations  13.4 us (6%)
  local copies, waits for them, and re-layouts  10.8 us (5%)
  other arithmetic  4.87 us (2%)
    psum x1, waiting for transfers between devices, reduce_amplitudes(): kernel = lax.psum(kernel_part, 'aux')  84.2 us
    all_to_all x1, blocking collectives, on_device(): lax.all_to_all(outgoing, 'orb', split_axis=0, concat_axis=0, tiled=True)  76.5 us
    dot_general x1, matrix products, accumulate(): jnp.einsum('si,sap->iap', pieces[2], product, precision=lax.Precision.HIG...  11.2 us
    dot_general x1, matrix products, accumulate(): jnp.einsum('sab,sbp->sap', pieces[0], pieces[1], preferred_element_type=j...  5.28 us
  transfers between devices with their start and end apart: 1, of which 1 were waited for; matrix products, arithmetic and copies ran while one was open for 1% of the time, Pallas kernels for 0%

commit v1 on v0

--- a/solution.py
+++ b/solution.py
@@ -10,7 +10,9 @@
 
 
 def reduce_amplitudes(kernel_part, own_rows, far_rows, weights, excitation):
-    kernel = lax.psum(kernel_part, "aux")
+    kernel = kernel_part
+    for hop in (1, 2):
+        kernel = kernel + lax.ppermute(kernel, "aux", [(dev, dev ^ hop) for dev in range(4)])
     return amplitudes(kernel, own_rows, far_rows, weights, excitation)
 
 

time: 210 us -> 248 us (1.18)
  waiting for transfers between devices: 84.2 us -> 133 us
  between operations: 13.4 us -> 0.05 us
  starting transfers between devices: 0.01 us -> 4.17 us
    ppermute x0 -> x2, waiting for transfers between devices: none -> 133 us  [reduce_amplitudes(): lax.ppermute(kernel, 'aux', [(dev, dev ^ hop) for dev in range(4)])]
    psum x1 -> x0, waiting for transfers between devices: 84.2 us -> none  [reduce_amplitudes(): kernel = lax.psum(kernel_part, 'aux')]
    ppermute x0 -> x2, starting transfers between devices: none -> 4.17 us  [reduce_amplitudes(): lax.ppermute(kernel, 'aux', [(dev, dev ^ hop) for dev in range(4)])]
  transfers between devices with their start and end apart: 1 -> 2, of which waited for: 1 -> 2; matrix products, arithmetic and copies ran while one was open for 1% -> 1% of each run, Pallas kernels for 0% -> 0%
where the time goes in v1:
time: 248 us
  waiting for transfers between devices  133 us (54%)
  blocking collectives  76.5 us (31%)
  matrix products  18.9 us (8%)
  local copies, waits for them, and re-layouts  8.98 us (4%)
  other arithmetic  6.52 us (3%)
  starting transfers between devices  4.17 us (2%)
    ppermute x2, waiting for transfers between devices, reduce_amplitudes(): lax.ppermute(kernel, 'aux', [(dev, dev ^ hop) for dev in range(4)])  133 us
    all_to_all x1, blocking collectives, on_device(): lax.all_to_all(outgoing, 'orb', split_axis=0, concat_axis=0, tiled=True)  76.5 us
    dot_general x1, matrix products, accumulate(): jnp.einsum('si,sap->iap', pieces[2], product, precision=lax.Precision.HIG...  11.2 us
    dot_general x1, matrix products, accumulate(): jnp.einsum('sab,sbp->sap', pieces[0], pieces[1], preferred_element_type=j...  5.91 us
  transfers between devices with their start and end apart: 2, of which 2 were waited for; matrix products, arithmetic and copies ran while one was open for 1% of the time, Pallas kernels for 0%

profile of v1, /device:TPU:0, one launch (start us, length us, event | category | flops | bytes accessed | tf_op | source)
XLA Modules:
  0.0 247.8 jit_solution(17168872518858006059)
XLA Ops:
  0.0 0.0 copy-start
  0.0 0.9 constant_dynamic-slice_fusion.2
  0.9 0.1 copy.8
  1.0 0.7 fusion.17
  1.7 0.2 copy-done
  1.9 3.6 %gather_fusion = bf16[8,256,1536]{2,1,0:T(8,128)(2,1)} fusion(bf16[4,256,1536]{2,1,0:T(8,128)(2,1)S(1)} %copy-done, s32[1024]{0:T(1024)S(1)} %pad_clamp_fusion.2), kind=kCustom, calls=%fused_computation | custom fusion | bytes 12582944 | tf_op jit(solution)/shard_map/jit(_take)/gather | solution.py:29
  5.5 3.5 %broadcast_select_fusion = bf16[8,256,1536]{2,1,0:T(8,128)(2,1)S(1)} fusion(bf16[8,256,1536]{2,1,0:T(8,128)(2,1)} %gather_fusion, pred[8]{0:T(512)(128)(4,1)S(1)} %and_bitcast_fusion), kind=kLoop, calls=%fused_computation.5 | loop fusion | flops 3145728 | bytes 12582920 | tf_op jit(solution)/shard_map/jit(_take)/select_n | solution.py:29
  9.0 76.5 %all_to_all.5 = bf16[8,256,1536]{2,1,0:T(8,128)(2,1)S(1)} all-to-all(bf16[8,256,1536]{2,1,0:T(8,128)(2,1)S(1)} %broadcast_select_fusion), channel_id=1, replica_groups=mesh['orb'=8,'aux'=4] {'orb'}, dimensions={0} | all-to-all | bytes 12582912 | tf_op jit(solution)/shard_map/all_to_all | solution.py:30
  85.5 0.0 copy-start.1
  85.5 1.8 fusion.20
  87.3 0.8 copy-done.1
  88.1 0.0 copy-start.2
  88.1 1.6 collective-permute-start
  89.7 45.1 %collective-permute-done = f32[8,256,256]{2,1,0:T(8,128)S(1)} collective-permute-done((f32[8,256,256]{2,1,0:T(8,128)S(1)}, f32[8,256,256]{2,1,0:T(8,128)S(1)}, u32[]{:S(2)}, u32[]{:S(2)}) %collective-permute-start) | collective-permute-done | bytes 2097184 | tf_op jit(solution)/shard_map/ppermute | solution.py:15
  134.8 1.7 add.67
  136.5 2.6 %collective-permute-start.1 = (f32[8,256,256]{2,1,0:T(8,128)}, f32[8,256,256]{2,1,0:T(8,128)}, u32[]{:S(2)}, u32[]{:S(2)}) collective-permute-start(f32[8,256,256]{2,1,0:T(8,128)} %add.67), channel_id=1, source_target_pairs={{0,2},{1,3},{2,0},{3,1},{4,6},{5,7},{6,4},{7,5},{8,10},{9,11},{10,... | collective-permute-start | bytes 6291464 | tf_op jit(solution)/shard_map/ppermute | solution.py:15
  139.1 0.0 copy-done.2
  139.1 0.6 gather_fusion.1
  139.7 0.6 gather_fusion.2
  140.2 0.7 fusion.14
  140.9 87.5 %collective-permute-done.1 = f32[8,256,256]{2,1,0:T(8,128)} collective-permute-done((f32[8,256,256]{2,1,0:T(8,128)}, f32[8,256,256]{2,1,0:T(8,128)}, u32[]{:S(2)}, u32[]{:S(2)}) %collective-permute-start.1) | collective-permute-done | bytes 2097184 | tf_op jit(solution)/shard_map/ppermute | solution.py:15
  228.4 5.9 %fusion.5 = f32[8,256,1536]{2,1,0:T(8,128)S(1)} fusion(bf16[8,256,1536]{2,1,0:T(8,128)(2,1)} %copy-done.1, f32[8,256,256]{2,1,0:T(8,128)} %add.67, f32[8,256,256]{2,1,0:T(8,128)} %collective-permute-done.1, f32[8,256]{1,0:T(8,128)S(1)} %gather_fusion.2, f32[8,256]{1,0:T(8,128)S(1)} %gather_fusion.1, f32[8]{0:T(128)S(1)} %fusion.14), kind=kOutput, calls=%fused_computation.8 | convolution fusion | flops 1613234176 | bytes 23085088 | tf_op jit(solution)/shard_map/while/body/eval_jaxpr/sab,sbp->sap/dot_general | solution.py:43
  234.4 11.2 %fusion.2 = bf16[4,256,1536]{2,0,1:T(4,128)(2,1)S(1)} fusion(f32[8,256,1536]{2,1,0:T(8,128)S(1)} %fusion.5, s32[8]{0:T(128)S(1)} %bitcast.25), kind=kOutput, calls=%fused_computation.6 | convolution fusion | flops 152567840 | bytes 15728672 | tf_op jit(solution)/shard_map/while/body/eval_jaxpr/si,sap->iap/dot_general | solution.py:46
  245.6 2.2 copy.6
  (4 shorter events, 0.0 us)
Async XLA Ops:
  0.0 1.9 copy-start
  85.5 2.6 %copy-start.1 = (bf16[8,256,1536]{2,1,0:T(8,128)(2,1)}, bf16[8,256,1536]{2,1,0:T(8,128)(2,1)S(1)}, u32[]{:S(2)}) copy-start(bf16[8,256,1536]{2,1,0:T(8,128)(2,1)S(1)} %all_to_all.5) | copy-start | bytes 18874372
  88.1 51.0 %copy-start.2 = (f32[32,256]{1,0:T(8,128)S(1)}, f32[32,256]{1,0:T(8,128)}, u32[]{:S(2)}) copy-start(f32[32,256]{1,0:T(8,128)} %param.5) | copy-start | bytes 98308
  88.1 46.7 %collective-permute-start = (f32[8,256,256]{2,1,0:T(8,128)S(1)}, f32[8,256,256]{2,1,0:T(8,128)S(1)}, u32[]{:S(2)}, u32[]{:S(2)}) collective-permute-start(f32[8,256,256]{2,1,0:T(8,128)S(1)} %fusion.20), channel_id=1, source_target_pairs={{0,1},{1,0},{2,3},{3,2},{4,5},{5,4},{6,7},{7,6},{8,9},{9,8},{10,11... | collective-permute-start | bytes 6291464 | tf_op jit(solution)/shard_map/ppermute | solution.py:15
  136.5 92.0 %collective-permute-start.1 = (f32[8,256,256]{2,1,0:T(8,128)}, f32[8,256,256]{2,1,0:T(8,128)}, u32[]{:S(2)}, u32[]{:S(2)}) collective-permute-start(f32[8,256,256]{2,1,0:T(8,128)} %add.67), channel_id=1, source_target_pairs={{0,2},{1,3},{2,0},{3,1},{4,6},{5,7},{6,4},{7,5},{8,10},{9,11},{10,... | collective-permute-start | bytes 6291464 | tf_op jit(solution)/shard_map/ppermute | solution.py:15
